TPU v7x, 256 devices: a whole 4x4x8 slice. The times are simulated.
256 devices in a mesh: depth: 16 (over x_hi, y, core), strip: 16 (over x_lo, z).
Axes of the slice: x: 4 (x_hi: 2, x_lo: 2; x = x_hi * 2 + x_lo), y: 4, z: 8, core: 2. Of those that a mesh axis runs over, the one named last changes fastest.
Arguments:
- volume: float32 [64, 1920, 1920], P('depth', 'strip'), may hold values from 0.001 to 4
- measured: float32 [1920, 1920], P('strip'), may hold values from 0.064 to 0.64
- row_taps: float32 [64, 31], P('depth'), may hold values from 0.009677419 to 0.09677419
- col_taps: float32 [64, 15, 31], P('depth'), may hold values from 0.009677419 to 0.09677419
- phase_map: int32 [64, 15], P('depth'), may hold values from 0 to 14
- radius: int32 [64], P('depth'), may hold values from 1 to 15, as said below
Outputs:
- volume_out: float32 [64, 1920, 1920], P('depth', 'strip')
Inputs may be any that keep to these rules, and one draw needn't show every extreme that they name: Some plane's radius is exactly 15.
All inputs are finite; a program needn't handle non-finite values.
Results may differ from a plain program's by a relative error of at most 0.0032.
Values may be sent and summed in bfloat16 or wider, within the bound.
A program may use at most 128 MiB of HBM per device.

v0:
```python
import functools

import jax
import jax.numpy as jnp
from jax import lax
from jax.experimental import pallas as pl
from jax.experimental.pallas import tpu as pltpu
from jax.sharding import PartitionSpec as P

PITCH = 15
RMAX = 15
TAPS = 2 * RMAX + 1
ITERS = 2
LANE = 128
WIN = 256
BW = 225
HALO = 16
MESH = pl.DeviceIdType.MESH
BF = jnp.bfloat16
F32 = jnp.float32


def iota(shape, axis):
    return lax.broadcasted_iota(jnp.int32, shape, axis)


def dot(a, b):
    return jnp.dot(a, b, preferred_element_type=F32)


def unwindow(ref, k, rows):
    b0, l0 = divmod(LANE * k, BW)
    n0 = min(LANE, BW - l0)
    base = WIN * b0
    if l0 == 0:
        a = ref[:rows, base : base + LANE]
    elif l0 < LANE:
        a = pltpu.roll(ref[:rows, base : base + WIN], WIN - l0, axis=1)[:, :LANE]
    elif l0 == LANE:
        a = ref[:rows, base + LANE : base + WIN]
    else:
        a = pltpu.roll(ref[:rows, base + LANE : base + WIN], WIN - l0, axis=1)
    if n0 < LANE:
        b = pltpu.roll(ref[:rows, base + WIN : base + WIN + LANE], n0, axis=1)
        a = jnp.where(iota(a.shape, 1) < n0, a, b)
    return a


def kernel(depths, strips, vol_hbm, meas_hbm, rt_ref, ct_ref, pm_ref, rad_ref, out_hbm,
           v32, spr, pw, pc, sb, qb, rb, s_ref, hs, hb, mc, rc, wr, ga, bpw,
           ctf, up, fm, gm, bt, bfm, cinv, rinv,
           sem_vol, sem_out, sem_mc, sem_ms, sem_mr, sem_ps, sem_pr, sem_rs, sem_rr,
           sem_hs, sem_hr, sem_as, sem_ar, sem_fs, sem_fr):
    planes, rows, cols = vol_hbm.shape
    ext = rows + 2 * HALO
    kext = ga.shape[0]
    nb = -(-cols // BW)
    nk = cols // LANE
    chips = depths // 2
    d = lax.axis_index("depth")
    s = lax.axis_index("strip")
    c = lax.rem(d, 2)
    chip = d // 2
    sibling = d + 1 - 2 * c
    above = lax.rem(s + strips - 1, strips)
    below = lax.rem(s + 1, strips)
    peers = [lax.rem(chip + r, chips) for r in range(chips)]
    givers = [lax.rem(chip + chips - r, chips) for r in range(chips)]

    vol_in = []
    for z in range(planes):
        copy = pltpu.make_async_copy(
            vol_hbm.at[z], v32.at[z, 0:rows, LANE : LANE + cols], sem_vol.at[z]
        )
        copy.start()
        vol_in.append(copy)
    col0 = pl.multiple_of(jnp.minimum(d, nk - 1) * LANE, LANE)
    mc_in = pltpu.make_async_copy(
        meas_hbm.at[:, pl.ds(col0, LANE)], mc.at[HALO : HALO + rows, :], sem_mc
    )
    mc_in.start()

    barrier = pltpu.get_barrier_semaphore()
    pl.semaphore_signal(barrier, inc=1, device_id={"depth": sibling}, device_id_type=MESH)
    for r in range(1, chips):
        pl.semaphore_signal(
            barrier, inc=1, device_id={"depth": 2 * peers[r] + c}, device_id_type=MESH
        )
    for t in (above, below):
        pl.semaphore_signal(barrier, inc=1, device_id={"strip": t}, device_id_type=MESH)

    for z in range(planes):
        v32[z, rows:, :] = jnp.zeros((LANE - rows, v32.shape[2]), F32)
        v32[z, :, 0:LANE] = jnp.zeros((LANE, LANE), F32)
        v32[z, :, LANE + cols :] = jnp.zeros((LANE, v32.shape[2] - LANE - cols), F32)
    for it in range(ITERS):
        pc[it, nk] = jnp.zeros((ext, LANE), BF)
        rc[it, 0] = jnp.zeros((kext, LANE), BF)
        for k in range(1, nk + 2):
            rc[it, k, ext:, :] = jnp.zeros((kext - ext, LANE), BF)

    up[...] = jnp.zeros_like(up)
    every = jnp.where(lax.rem(iota((WIN, LANE), 0), PITCH) == iota((WIN, LANE), 1), 1.0, 0.0)
    every = every.astype(BF)
    inside = s * rows - HALO + iota((WIN, LANE), 0)
    inside = jnp.where((inside >= 0) & (inside < rows * strips), 1.0, 0.0).astype(BF)
    xs = BW * iota((16, WIN), 0) - RMAX + iota((16, WIN), 1)
    ones_win = jnp.where((xs >= 0) & (xs < cols), 1.0, 0.0).astype(BF)
    xo = BW * iota((16, WIN), 0) + iota((16, WIN), 1)
    col_ok = (xo < cols) & (iota((16, WIN), 1) < BW)
    row_ok = iota((LANE, LANE), 0) < rows
    for z in range(planes):
        reach = rad_ref[z]
        ctf[...] = jnp.zeros_like(ctf)
        keep = jnp.abs(iota((PITCH, TAPS), 1) - RMAX) <= reach
        ctf[0:PITCH, 0:TAPS] = jnp.where(keep, ct_ref[z], 0.0)
        keep1 = jnp.abs(iota((1, TAPS), 1) - RMAX) <= reach
        ctf[16:17, 0:TAPS] = jnp.where(keep1, rt_ref[z : z + 1, :], 0.0)
        family = jnp.full((16, LANE), -1, jnp.int32)
        for p in range(PITCH):
            family = jnp.where(iota((16, LANE), 0) == p, pm_ref[z, p], family)
        pick = jnp.where(family == iota((16, LANE), 1), 1.0, 0.0).astype(BF)
        table = ctf[...].astype(BF)
        up[0:16, :] = dot(pick, table)
        taps = dot(every, up[...].astype(BF))
        taps = jnp.concatenate([taps, jnp.zeros((WIN, WIN - LANE), F32)], axis=1)
        fwd = pltpu.roll(taps, 32 - 2 * RMAX, axis=1)
        fwd = pltpu.roll(fwd, WIN - 32, axis=1, stride=1, stride_axis=0)
        fm[z] = fwd.astype(BF)
        back = pltpu.roll(taps, 0, axis=1, stride=1, stride_axis=0)
        gm[z] = jnp.transpose(back).astype(BF)
        rtap = jnp.concatenate([ctf[16:17, :], jnp.zeros((1, WIN - LANE), F32)], axis=1)
        rtap = jnp.broadcast_to(rtap, (LANE, WIN))
        band = pltpu.roll(rtap, 1, axis=1)
        band = pltpu.roll(band, 0, axis=1, stride=1, stride_axis=0)
        bt[z] = band[:, :kext].astype(BF)
        bfm[:, LANE * z : LANE * (z + 1)] = jnp.transpose(band)[:kext, :].astype(BF)
        rn = dot(band.astype(BF), inside)
        rinv[z] = jnp.where(row_ok, 1.0 / rn, 0.0)
        cn = dot(ones_win, gm[z])
        cinv[z] = jnp.where(col_ok, 1.0 / cn, 0.0)

    pl.semaphore_wait(barrier, chips + 2)
    mc_in.wait()
    m_up = pltpu.make_async_remote_copy(
        src_ref=mc.at[HALO : 2 * HALO, :], dst_ref=mc.at[HALO + rows : ext, :],
        send_sem=sem_ms.at[0], recv_sem=sem_mr.at[0],
        device_id={"strip": above}, device_id_type=MESH,
    )
    m_down = pltpu.make_async_remote_copy(
        src_ref=mc.at[rows : rows + HALO, :], dst_ref=mc.at[0:HALO, :],
        send_sem=sem_ms.at[1], recv_sem=sem_mr.at[1],
        device_id={"strip": below}, device_id_type=MESH,
    )
    m_up.start()
    m_down.start()
    for copy in vol_in:
        copy.wait()

    def window(z, b):
        q, sh = divmod(LANE - RMAX + BW * b, LANE)
        x = v32[z, :, LANE * q : LANE * q + WIN + LANE]
        if sh:
            x = pltpu.roll(x, WIN + LANE - sh, axis=1)
        return x[:, :WIN].astype(BF)

    out_copies = []
    for it in range(ITERS):
        @pl.loop(0, planes)
        def _(z):
            for g in range(0, nb, 3):
                lhs = jnp.concatenate([window(z, b) for b in range(g, g + 3)], axis=0)
                res = dot(lhs, fm[z])
                for i in range(3):
                    spr[pl.ds(pl.multiple_of(z * LANE, LANE), LANE),
                        WIN * (g + i) : WIN * (g + i + 1)] = (
                        res[LANE * i : LANE * (i + 1)].astype(BF)
                    )

        pair = []
        done = 0
        for b in range(nb):
            pw[:, WIN * b : WIN * (b + 1)] = dot(bfm[...], spr[:, WIN * b : WIN * (b + 1)])
            while done < nk and (LANE * (done + 1) <= BW * (b + 1) or b == nb - 1):
                pc[it, done] = unwindow(pw, done, ext).astype(BF)
                done += 1
                if done % 2 == 0 or done == nk:
                    m = (done - 1) // 2
                    copy = pltpu.make_async_remote_copy(
                        src_ref=pc.at[it, 2 * m + 1 - c], dst_ref=sb.at[it, m],
                        send_sem=sem_ps.at[it, m], recv_sem=sem_pr.at[it, m],
                        device_id={"depth": sibling}, device_id_type=MESH,
                    )
                    copy.start()
                    pair.append(copy)

        for copy in pair:
            copy.wait_recv()
        spread_out = []
        for r in range(1, chips):
            k = peers[r]
            qb[it, r] = (pc[it, 2 * k + c].astype(F32) + sb[it, k].astype(F32)).astype(BF)
            copy = pltpu.make_async_remote_copy(
                src_ref=qb.at[it, r], dst_ref=rb.at[it, r],
                send_sem=sem_rs.at[it, r], recv_sem=sem_rr.at[it, r],
                device_id={"depth": 2 * k + c}, device_id_type=MESH,
            )
            copy.start()
            spread_out.append(copy)
        total = pc[it, d].astype(F32) + sb[it, chip].astype(F32)
        for copy in spread_out:
            copy.wait_recv()
        for r in range(1, chips):
            total = total + rb[it, r].astype(F32)
        s_ref[...] = total

        hs[it, 0] = s_ref[0 : 2 * HALO, :]
        hs[it, 1] = s_ref[rows:ext, :]
        h_up = pltpu.make_async_remote_copy(
            src_ref=hs.at[it, 0], dst_ref=hb.at[it, 1],
            send_sem=sem_hs.at[it, 0], recv_sem=sem_hr.at[it, 0],
            device_id={"strip": above}, device_id_type=MESH,
        )
        h_down = pltpu.make_async_remote_copy(
            src_ref=hs.at[it, 1], dst_ref=hb.at[it, 0],
            send_sem=sem_hs.at[it, 1], recv_sem=sem_hr.at[it, 1],
            device_id={"strip": below}, device_id_type=MESH,
        )
        h_up.start()
        h_down.start()
        if it == 0:
            m_up.wait()
            m_down.wait()
        h_up.wait()
        h_down.wait()
        s_ref[0 : 2 * HALO, :] = s_ref[0 : 2 * HALO, :] + jnp.where(s > 0, hb[it, 0], 0.0)
        s_ref[rows:ext, :] = s_ref[rows:ext, :] + jnp.where(s < strips - 1, hb[it, 1], 0.0)
        y = s * rows - HALO + iota((ext, LANE), 0)
        ok = (y >= 0) & (y < rows * strips) & (d < nk)
        rc[it, 1 + d, 0:ext, :] = jnp.where(ok, mc[...] / s_ref[...], 0.0).astype(BF)

        def give(slot, target, send, recv):
            return pltpu.make_async_remote_copy(
                src_ref=rc.at[it, slot, 0:ext, :], dst_ref=rc.at[it, slot, 0:ext, :],
                send_sem=send, recv_sem=recv,
                device_id={"depth": target}, device_id_type=MESH,
            )

        sent = []
        for r in range(1, chips):
            copy = give(1 + d, 2 * peers[r] + c, sem_as.at[it, r], sem_ar.at[it, r])
            copy.start()
            sent.append(copy)
        copy = give(1 + d, sibling, sem_fs.at[it, 0], sem_fr.at[it, 0])
        copy.start()
        sent.append(copy)
        for r in range(1, chips):
            slot = 1 + 2 * givers[r] + c
            give(slot, sibling, sem_as.at[it, r], sem_ar.at[it, r]).wait_recv()
            copy = give(slot, sibling, sem_fs.at[it, r], sem_fr.at[it, r])
            copy.start()
            sent.append(copy)
        for r in range(chips):
            slot = 1 + 2 * givers[r] + 1 - c
            give(slot, sibling, sem_fs.at[it, r], sem_fr.at[it, r]).wait_recv()

        for b in range(nb):
            q, sh = divmod(LANE - RMAX + BW * b, LANE)
            x = jnp.concatenate([rc[it, q + i].astype(F32) for i in range(3)], axis=1)
            if sh:
                x = pltpu.roll(x, WIN + LANE - sh, axis=1)
            wr[kext * b : kext * (b + 1), :] = x[:, :WIN].astype(BF)

        @pl.loop(0, planes)
        def _(z):
            for g in range(0, nb, 3):
                res = dot(wr[kext * g : kext * (g + 3), :], gm[z])
                for i in range(3):
                    ga[:, WIN * (g + i) : WIN * (g + i + 1)] = (
                        res[kext * i : kext * (i + 1)].astype(BF)
                    )
            scale = jnp.concatenate([rinv[z], rinv[z]], axis=1)
            for b in range(nb):
                bp = dot(bt[z], ga[:, WIN * b : WIN * (b + 1)])
                bpw[:, WIN * b : WIN * (b + 1)] = bp * scale * cinv[z, b : b + 1, :]
            for k in range(nk):
                at = slice(LANE * (k + 1), LANE * (k + 2))
                v32[z, :, at] = v32[z, :, at] * unwindow(bpw, k, LANE)
            if it == ITERS - 1:
                pltpu.make_async_copy(
                    v32.at[z, 0:rows, LANE : LANE + cols], out_hbm.at[z], sem_out.at[z]
                ).start()

        out_copies += pair + spread_out + sent

    for copy in out_copies:
        copy.wait_send()
    for z in range(planes):
        pltpu.make_async_copy(
            v32.at[z, 0:rows, LANE : LANE + cols], out_hbm.at[z], sem_out.at[z]
        ).wait()


def local(depths, strips, volume, measured, row_taps, col_taps, phase_map, radius):
    planes, rows, cols = volume.shape
    ext = rows + 2 * HALO
    kext = 160
    nb = -(-cols // BW)
    nk = cols // LANE
    chips = depths // 2
    dma = pltpu.SemaphoreType.DMA
    vmem = pltpu.VMEM
    return pl.pallas_call(
        functools.partial(kernel, depths, strips),
        out_shape=jax.ShapeDtypeStruct(volume.shape, F32),
        in_specs=[
            pl.BlockSpec(memory_space=pl.ANY),
            pl.BlockSpec(memory_space=pl.ANY),
            pl.BlockSpec(memory_space=pltpu.VMEM),
            pl.BlockSpec(memory_space=pltpu.VMEM),
            pl.BlockSpec(memory_space=pltpu.SMEM),
            pl.BlockSpec(memory_space=pltpu.SMEM),
        ],
        out_specs=pl.BlockSpec(memory_space=pl.ANY),
        scratch_shapes=[
            vmem((planes, LANE, cols + 2 * LANE), F32),
            vmem((planes * LANE, nb * WIN), BF),
            vmem((kext, nb * WIN), F32),
            vmem((ITERS, nk + 1, ext, LANE), BF),
            vmem((ITERS, chips, ext, LANE), BF),
            vmem((ITERS, chips, ext, LANE), BF),
            vmem((ITERS, chips, ext, LANE), BF),
            vmem((ext, LANE), F32),
            vmem((ITERS, 2, 2 * HALO, LANE), F32),
            vmem((ITERS, 2, 2 * HALO, LANE), F32),
            vmem((ext, LANE), F32),
            vmem((ITERS, nk + 2, kext, LANE), BF),
            vmem((nb * kext, WIN), BF),
            vmem((kext, nb * WIN), BF),
            vmem((LANE, nb * WIN), F32),
            vmem((LANE, LANE), F32),
            vmem((LANE, LANE), F32),
            vmem((planes, WIN, WIN), BF),
            vmem((planes, WIN, WIN), BF),
            vmem((planes, LANE, kext), BF),
            vmem((kext, planes * LANE), BF),
            vmem((planes, 16, WIN), F32),
            vmem((planes, LANE, LANE), F32),
            dma((planes,)),
            dma((planes,)),
            dma,
            dma((2,)),
            dma((2,)),
            dma((ITERS, chips)),
            dma((ITERS, chips)),
            dma((ITERS, chips)),
            dma((ITERS, chips)),
            dma((ITERS, 2)),
            dma((ITERS, 2)),
            dma((ITERS, chips)),
            dma((ITERS, chips)),
            dma((ITERS, chips)),
            dma((ITERS, chips)),
        ],
        compiler_params=pltpu.CompilerParams(
            collective_id=0, has_side_effects=True, vmem_limit_bytes=48 * 1024 * 1024
        ),
    )(volume, measured, row_taps, col_taps, phase_map, radius)


def solution(mesh):
    return jax.shard_map(
        functools.partial(local, mesh.shape["depth"], mesh.shape["strip"]),
        mesh=mesh,
        in_specs=(
            P("depth", "strip", None),
            P("strip", None),
            P("depth", None),
            P("depth", None, None),
            P("depth", None),
            P("depth"),
        ),
        out_specs=P("depth", "strip", None),
        check_vma=False,
    )
```

profile of v0, /device:TPU:1, one launch (start us, length us, event | category | flops | bytes accessed | tf_op | source)
XLA Modules:
  0.0 71.6 jit_solution(15611732706424687547)
XLA Ops:
  0.0 0.8 %copy.7.ct_ref = f32[4,15,31]{2,1,0:T(8,128)S(1)} copy(f32[4,15,31]{2,0,1:T(4,128)} %param.9) | data formatting | bytes 14880 | tf_op args[3]
  0.8 0.0 copy-start
  0.8 1.2 %copy-done = f32[120,1920]{1,0:T(8,128)S(1)} copy-done((f32[120,1920]{1,0:T(8,128)S(1)}, f32[120,1920]{1,0:T(8,128)}, u32[]{:S(2)}) %copy-start) | copy-done | bytes 921624
  1.9 0.0 copy-start.1
  1.9 0.7 copy-done.1
  2.6 0.0 copy-start.2
  2.6 0.7 copy-done.2
  3.3 0.0 copy-start.3
  3.3 0.7 copy-done.3
  4.0 65.8 %shard_map.64 = f32[4,120,1920]{2,1,0:T(8,128)S(1)} custom-call(f32[4,120,1920]{2,1,0:T(8,128)} %vol_hbm.1, f32[120,1920]{1,0:T(8,128)S(1)} %copy-done, f32[4,31]{1,0:T(4,128)S(1)} %copy-done.1, f32[4,15,31]{2,1,0:T(8,128)S(1)} %copy.7.ct_ref, s32[4,15]{1,0:T(4,128)S(1)} %copy-done.2, s32[4]{0:T(128)S(1)} %copy-done.3), custom_call_target="tpu_custom_call" | custom-call | tf_op jit(solution)/shard_map/pallas_call | solution.py:313
  69.8 1.8 %copy.9 = f32[4,120,1920]{2,1,0:T(8,128)} copy(f32[4,120,1920]{2,1,0:T(8,128)S(1)} %shard_map.64) | data formatting | bytes 7372800
Async XLA Ops:
  0.8 1.2 %copy-start = (f32[120,1920]{1,0:T(8,128)S(1)}, f32[120,1920]{1,0:T(8,128)}, u32[]{:S(2)}) copy-start(f32[120,1920]{1,0:T(8,128)} %meas_hbm.1) | copy-start | bytes 2764804
  1.9 0.7 copy-start.1
  2.6 0.7 copy-start.2
  3.3 0.7 copy-start.3
where the time goes:
time: 71.9 us; the launch traced here: 71.6 us
  Pallas kernels  65.8 us (92%)
  local copies, waits for them, and re-layouts  5.8 us (8%)
    pallas_call x1, Pallas kernels, local(): pl.pallas_call(functools.partial(kernel, depths, strips), out_shape=jax.S...  65.8 us
    unnamed x10, local copies, waits for them, and re-layouts  5.8 us

commit v1 on v0

--- a/solution.py
+++ b/solution.py
@@ -46,14 +46,16 @@
     return a
 
 
-def kernel(depths, strips, vol_hbm, meas_hbm, rt_ref, ct_ref, pm_ref, rad_ref, out_hbm,
-           v32, spr, pw, pc, sb, qb, rb, s_ref, hs, hb, mc, rc, wr, ga, bpw,
+def kernel(depths, strips, vol_hbm, meas_hbm, rt_hbm, ct_hbm, pm_hbm, rad_hbm, out_hbm,
+           rt_ref, ct_ref, pm_ref, rad_ref,
+           v32, spr, pw, pc, sb, qb, rb, s_ref, hb, mc, rc, wr, ga, bpw,
            ctf, up, fm, gm, bt, bfm, cinv, rinv,
-           sem_vol, sem_out, sem_mc, sem_ms, sem_mr, sem_ps, sem_pr, sem_rs, sem_rr,
+           sem_vol, sem_out, sem_in, sem_ms, sem_mr, sem_ps, sem_pr, sem_rs, sem_rr,
            sem_hs, sem_hr, sem_as, sem_ar, sem_fs, sem_fr):
     planes, rows, cols = vol_hbm.shape
     ext = rows + 2 * HALO
-    kext = ga.shape[0]
+    kext = ga.shape[1]
+    edge = 4 * HALO
     nb = -(-cols // BW)
     nk = cols // LANE
     chips = depths // 2
@@ -67,6 +69,16 @@
     peers = [lax.rem(chip + r, chips) for r in range(chips)]
     givers = [lax.rem(chip + chips - r, chips) for r in range(chips)]
 
+    def strip_row(p):
+        return jnp.where(p < 2 * HALO, p + rows - HALO, p - 3 * HALO)
+
+    arg_in = []
+    for i, (src, dst) in enumerate(
+        ((rt_hbm, rt_ref), (ct_hbm, ct_ref), (pm_hbm, pm_ref), (rad_hbm, rad_ref))
+    ):
+        copy = pltpu.make_async_copy(src, dst, sem_in.at[i])
+        copy.start()
+        arg_in.append(copy)
     vol_in = []
     for z in range(planes):
         copy = pltpu.make_async_copy(
@@ -75,10 +87,16 @@
         copy.start()
         vol_in.append(copy)
     col0 = pl.multiple_of(jnp.minimum(d, nk - 1) * LANE, LANE)
-    mc_in = pltpu.make_async_copy(
-        meas_hbm.at[:, pl.ds(col0, LANE)], mc.at[HALO : HALO + rows, :], sem_mc
-    )
-    mc_in.start()
+    mc_in = [
+        pltpu.make_async_copy(
+            meas_hbm.at[0 : rows - HALO, pl.ds(col0, LANE)], mc.at[3 * HALO : ext, :], sem_in.at[4]
+        ),
+        pltpu.make_async_copy(
+            meas_hbm.at[rows - HALO : rows, pl.ds(col0, LANE)], mc.at[0:HALO, :], sem_in.at[5]
+        ),
+    ]
+    for copy in mc_in:
+        copy.start()
 
     barrier = pltpu.get_barrier_semaphore()
     pl.semaphore_signal(barrier, inc=1, device_id={"depth": sibling}, device_id_type=MESH)
@@ -102,18 +120,21 @@
     up[...] = jnp.zeros_like(up)
     every = jnp.where(lax.rem(iota((WIN, LANE), 0), PITCH) == iota((WIN, LANE), 1), 1.0, 0.0)
     every = every.astype(BF)
-    inside = s * rows - HALO + iota((WIN, LANE), 0)
-    inside = jnp.where((inside >= 0) & (inside < rows * strips), 1.0, 0.0).astype(BF)
+    y = s * rows + strip_row(iota((kext, LANE), 0))
+    inside = (y >= 0) & (y < rows * strips) & (iota((kext, LANE), 0) < ext)
+    inside = jnp.where(inside, 1.0, 0.0).astype(BF)
     xs = BW * iota((16, WIN), 0) - RMAX + iota((16, WIN), 1)
     ones_win = jnp.where((xs >= 0) & (xs < cols), 1.0, 0.0).astype(BF)
     xo = BW * iota((16, WIN), 0) + iota((16, WIN), 1)
     col_ok = (xo < cols) & (iota((16, WIN), 1) < BW)
     row_ok = iota((LANE, LANE), 0) < rows
+    for copy in arg_in:
+        copy.wait()
     for z in range(planes):
         reach = rad_ref[z]
         ctf[...] = jnp.zeros_like(ctf)
         keep = jnp.abs(iota((PITCH, TAPS), 1) - RMAX) <= reach
-        ctf[0:PITCH, 0:TAPS] = jnp.where(keep, ct_ref[z], 0.0)
+        ctf[0:PITCH, 0:TAPS] = jnp.where(keep, ct_ref[:, z, :], 0.0)
         keep1 = jnp.abs(iota((1, TAPS), 1) - RMAX) <= reach
         ctf[16:17, 0:TAPS] = jnp.where(keep1, rt_ref[z : z + 1, :], 0.0)
         family = jnp.full((16, LANE), -1, jnp.int32)
@@ -133,22 +154,27 @@
         rtap = jnp.broadcast_to(rtap, (LANE, WIN))
         band = pltpu.roll(rtap, 1, axis=1)
         band = pltpu.roll(band, 0, axis=1, stride=1, stride_axis=0)
+        p = iota((LANE, WIN), 1)
+        last = pltpu.roll(band, WIN - rows, axis=1)
+        band = jnp.where(p < 2 * HALO, last, pltpu.roll(band, 2 * HALO, axis=1))
+        band = jnp.where(p < ext, band, 0.0)
         bt[z] = band[:, :kext].astype(BF)
         bfm[:, LANE * z : LANE * (z + 1)] = jnp.transpose(band)[:kext, :].astype(BF)
-        rn = dot(band.astype(BF), inside)
+        rn = dot(bt[z], inside)
         rinv[z] = jnp.where(row_ok, 1.0 / rn, 0.0)
         cn = dot(ones_win, gm[z])
         cinv[z] = jnp.where(col_ok, 1.0 / cn, 0.0)
 
     pl.semaphore_wait(barrier, chips + 2)
-    mc_in.wait()
+    for copy in mc_in:
+        copy.wait()
     m_up = pltpu.make_async_remote_copy(
-        src_ref=mc.at[HALO : 2 * HALO, :], dst_ref=mc.at[HALO + rows : ext, :],
+        src_ref=mc.at[3 * HALO : 4 * HALO, :], dst_ref=mc.at[HALO : 2 * HALO, :],
         send_sem=sem_ms.at[0], recv_sem=sem_mr.at[0],
         device_id={"strip": above}, device_id_type=MESH,
     )
     m_down = pltpu.make_async_remote_copy(
-        src_ref=mc.at[rows : rows + HALO, :], dst_ref=mc.at[0:HALO, :],
+        src_ref=mc.at[0:HALO, :], dst_ref=mc.at[2 * HALO : 3 * HALO, :],
         send_sem=sem_ms.at[1], recv_sem=sem_mr.at[1],
         device_id={"strip": below}, device_id_type=MESH,
     )
@@ -194,12 +220,18 @@
                     copy.start()
                     pair.append(copy)
 
-        for copy in pair:
-            copy.wait_recv()
+        def paired(m):
+            pltpu.make_async_remote_copy(
+                src_ref=pc.at[it, 2 * m + 1 - c], dst_ref=sb.at[it, m],
+                send_sem=sem_ps.at[it, m], recv_sem=sem_pr.at[it, m],
+                device_id={"depth": sibling}, device_id_type=MESH,
+            ).wait_recv()
+            return pc[it, 2 * m + c].astype(F32) + sb[it, m].astype(F32)
+
         spread_out = []
         for r in range(1, chips):
             k = peers[r]
-            qb[it, r] = (pc[it, 2 * k + c].astype(F32) + sb[it, k].astype(F32)).astype(BF)
+            qb[it, r] = paired(k).astype(BF)
             copy = pltpu.make_async_remote_copy(
                 src_ref=qb.at[it, r], dst_ref=rb.at[it, r],
                 send_sem=sem_rs.at[it, r], recv_sem=sem_rr.at[it, r],
@@ -207,81 +239,114 @@
             )
             copy.start()
             spread_out.append(copy)
-        total = pc[it, d].astype(F32) + sb[it, chip].astype(F32)
-        for copy in spread_out:
-            copy.wait_recv()
+        total = paired(chip)
         for r in range(1, chips):
+            spread_out[r - 1].wait_recv()
             total = total + rb[it, r].astype(F32)
-        s_ref[...] = total
-
-        hs[it, 0] = s_ref[0 : 2 * HALO, :]
-        hs[it, 1] = s_ref[rows:ext, :]
+        s_ref[it] = total
+
         h_up = pltpu.make_async_remote_copy(
-            src_ref=hs.at[it, 0], dst_ref=hb.at[it, 1],
+            src_ref=s_ref.at[it, 2 * HALO : edge], dst_ref=hb.at[it, 0 : 2 * HALO],
             send_sem=sem_hs.at[it, 0], recv_sem=sem_hr.at[it, 0],
             device_id={"strip": above}, device_id_type=MESH,
         )
         h_down = pltpu.make_async_remote_copy(
-            src_ref=hs.at[it, 1], dst_ref=hb.at[it, 0],
+            src_ref=s_ref.at[it, 0 : 2 * HALO], dst_ref=hb.at[it, 2 * HALO : edge],
             send_sem=sem_hs.at[it, 1], recv_sem=sem_hr.at[it, 1],
             device_id={"strip": below}, device_id_type=MESH,
         )
         h_up.start()
         h_down.start()
-        if it == 0:
-            m_up.wait()
-            m_down.wait()
-        h_up.wait()
-        h_down.wait()
-        s_ref[0 : 2 * HALO, :] = s_ref[0 : 2 * HALO, :] + jnp.where(s > 0, hb[it, 0], 0.0)
-        s_ref[rows:ext, :] = s_ref[rows:ext, :] + jnp.where(s < strips - 1, hb[it, 1], 0.0)
-        y = s * rows - HALO + iota((ext, LANE), 0)
-        ok = (y >= 0) & (y < rows * strips) & (d < nk)
-        rc[it, 1 + d, 0:ext, :] = jnp.where(ok, mc[...] / s_ref[...], 0.0).astype(BF)
-
-        def give(slot, target, send, recv):
+
+        def give(part, slot, target, send, recv):
+            at = rc.at[it, slot, edge:ext, :] if part == 0 else rc.at[it, slot, 0:edge, :]
             return pltpu.make_async_remote_copy(
-                src_ref=rc.at[it, slot, 0:ext, :], dst_ref=rc.at[it, slot, 0:ext, :],
-                send_sem=send, recv_sem=recv,
+                src_ref=at, dst_ref=at, send_sem=send, recv_sem=recv,
                 device_id={"depth": target}, device_id_type=MESH,
             )
 
         sent = []
-        for r in range(1, chips):
-            copy = give(1 + d, 2 * peers[r] + c, sem_as.at[it, r], sem_ar.at[it, r])
+
+        def give_own(part):
+            for r in range(1, chips):
+                copy = give(part, 1 + d, 2 * peers[r] + c,
+                            sem_as.at[it, part, r], sem_ar.at[it, part, r])
+                copy.start()
+                sent.append(copy)
+            copy = give(part, 1 + d, sibling, sem_fs.at[it, part, 0], sem_fr.at[it, part, 0])
             copy.start()
             sent.append(copy)
-        copy = give(1 + d, sibling, sem_fs.at[it, 0], sem_fr.at[it, 0])
-        copy.start()
-        sent.append(copy)
-        for r in range(1, chips):
-            slot = 1 + 2 * givers[r] + c
-            give(slot, sibling, sem_as.at[it, r], sem_ar.at[it, r]).wait_recv()
-            copy = give(slot, sibling, sem_fs.at[it, r], sem_fr.at[it, r])
-            copy.start()
-            sent.append(copy)
-        for r in range(chips):
-            slot = 1 + 2 * givers[r] + 1 - c
-            give(slot, sibling, sem_fs.at[it, r], sem_fr.at[it, r]).wait_recv()
-
-        for b in range(nb):
-            q, sh = divmod(LANE - RMAX + BW * b, LANE)
-            x = jnp.concatenate([rc[it, q + i].astype(F32) for i in range(3)], axis=1)
-            if sh:
-                x = pltpu.roll(x, WIN + LANE - sh, axis=1)
-            wr[kext * b : kext * (b + 1), :] = x[:, :WIN].astype(BF)
+
+        def forward(part):
+            for r in range(1, chips):
+                slot = 1 + 2 * givers[r] + c
+                give(part, slot, sibling,
+                     sem_as.at[it, part, r], sem_ar.at[it, part, r]).wait_recv()
+                copy = give(part, slot, sibling, sem_fs.at[it, part, r], sem_fr.at[it, part, r])
+                copy.start()
+                sent.append(copy)
+
+        def arrived(part):
+            for r in range(chips):
+                slot = 1 + 2 * givers[r] + 1 - c
+                give(part, slot, sibling,
+                     sem_fs.at[it, part, r], sem_fr.at[it, part, r]).wait_recv()
+
+        def back_windows(top, end):
+            for b in range(nb):
+                q, sh = divmod(LANE - RMAX + BW * b, LANE)
+                x = jnp.concatenate(
+                    [rc[it, q + i, top:end, :].astype(F32) for i in range(3)], axis=1
+                )
+                if sh:
+                    x = pltpu.roll(x, WIN + LANE - sh, axis=1)
+                wr[nb * top + (end - top) * b : nb * top + (end - top) * (b + 1), :] = (
+                    x[:, :WIN].astype(BF)
+                )
+
+        def back_columns(z, top, end):
+            n = end - top
+            for g in range(0, nb, 3):
+                res = dot(wr[nb * top + n * g : nb * top + n * (g + 3), :], gm[z])
+                for i in range(3):
+                    ga[z, top:end, WIN * (g + i) : WIN * (g + i + 1)] = (
+                        res[n * i : n * (i + 1)].astype(BF)
+                    )
+
+        if it == 0:
+            m_up.wait_recv()
+            m_down.wait_recv()
+        y = s * rows + strip_row(iota((ext, LANE), 0))
+        ok = (y >= 0) & (y < rows * strips) & (d < nk)
+        ratio = jnp.where(ok[edge:], mc[edge:, :] / s_ref[it, edge:, :], 0.0)
+        rc[it, 1 + d, edge:ext, :] = ratio.astype(BF)
+        give_own(0)
+        h_up.wait_recv()
+        h_down.wait_recv()
+        first = iota((edge, LANE), 0) < 2 * HALO
+        other = (first & (s < strips - 1)) | (~first & (s > 0))
+        shared = s_ref[it, 0:edge, :] + jnp.where(other, hb[it], 0.0)
+        ratio = jnp.where(ok[:edge], mc[0:edge, :] / shared, 0.0)
+        rc[it, 1 + d, 0:edge, :] = ratio.astype(BF)
+        give_own(1)
+        forward(0)
+        arrived(0)
+        back_windows(edge, kext)
+        forward(1)
 
         @pl.loop(0, planes)
         def _(z):
-            for g in range(0, nb, 3):
-                res = dot(wr[kext * g : kext * (g + 3), :], gm[z])
-                for i in range(3):
-                    ga[:, WIN * (g + i) : WIN * (g + i + 1)] = (
-                        res[kext * i : kext * (i + 1)].astype(BF)
-                    )
+            back_columns(z, edge, kext)
+
+        arrived(1)
+        back_windows(0, edge)
+
+        @pl.loop(0, planes)
+        def _(z):
+            back_columns(z, 0, edge)
             scale = jnp.concatenate([rinv[z], rinv[z]], axis=1)
             for b in range(nb):
-                bp = dot(bt[z], ga[:, WIN * b : WIN * (b + 1)])
+                bp = dot(bt[z], ga[z, :, WIN * b : WIN * (b + 1)])
                 bpw[:, WIN * b : WIN * (b + 1)] = bp * scale * cinv[z, b : b + 1, :]
             for k in range(nk):
                 at = slice(LANE * (k + 1), LANE * (k + 2))
@@ -291,9 +356,9 @@
                     v32.at[z, 0:rows, LANE : LANE + cols], out_hbm.at[z], sem_out.at[z]
                 ).start()
 
-        out_copies += pair + spread_out + sent
-
-    for copy in out_copies:
+        out_copies += pair + spread_out + sent + [h_up, h_down]
+
+    for copy in out_copies + [m_up, m_down]:
         copy.wait_send()
     for z in range(planes):
         pltpu.make_async_copy(
@@ -313,16 +378,13 @@
     return pl.pallas_call(
         functools.partial(kernel, depths, strips),
         out_shape=jax.ShapeDtypeStruct(volume.shape, F32),
-        in_specs=[
-            pl.BlockSpec(memory_space=pl.ANY),
-            pl.BlockSpec(memory_space=pl.ANY),
-            pl.BlockSpec(memory_space=pltpu.VMEM),
-            pl.BlockSpec(memory_space=pltpu.VMEM),
-            pl.BlockSpec(memory_space=pltpu.SMEM),
-            pl.BlockSpec(memory_space=pltpu.SMEM),
-        ],
+        in_specs=[pl.BlockSpec(memory_space=pltpu.HBM)] * 6,
         out_specs=pl.BlockSpec(memory_space=pl.ANY),
         scratch_shapes=[
+            vmem(row_taps.shape, F32),
+            vmem((PITCH, planes, TAPS), F32),
+            pltpu.SMEM(phase_map.shape, jnp.int32),
+            pltpu.SMEM(radius.shape, jnp.int32),
             vmem((planes, LANE, cols + 2 * LANE), F32),
             vmem((planes * LANE, nb * WIN), BF),
             vmem((kext, nb * WIN), F32),
@@ -330,13 +392,12 @@
             vmem((ITERS, chips, ext, LANE), BF),
             vmem((ITERS, chips, ext, LANE), BF),
             vmem((ITERS, chips, ext, LANE), BF),
-            vmem((ext, LANE), F32),
-            vmem((ITERS, 2, 2 * HALO, LANE), F32),
-            vmem((ITERS, 2, 2 * HALO, LANE), F32),
+            vmem((ITERS, ext, LANE), F32),
+            vmem((ITERS, 4 * HALO, LANE), F32),
             vmem((ext, LANE), F32),
             vmem((ITERS, nk + 2, kext, LANE), BF),
             vmem((nb * kext, WIN), BF),
-            vmem((kext, nb * WIN), BF),
+            vmem((planes, kext, nb * WIN), BF),
             vmem((LANE, nb * WIN), F32),
             vmem((LANE, LANE), F32),
             vmem((LANE, LANE), F32),
@@ -348,7 +409,7 @@
             vmem((planes, LANE, LANE), F32),
             dma((planes,)),
             dma((planes,)),
-            dma,
+            dma((6,)),
             dma((2,)),
             dma((2,)),
             dma((ITERS, chips)),
@@ -357,15 +418,18 @@
             dma((ITERS, chips)),
             dma((ITERS, 2)),
             dma((ITERS, 2)),
-            dma((ITERS, chips)),
-            dma((ITERS, chips)),
-            dma((ITERS, chips)),
-            dma((ITERS, chips)),
+            dma((ITERS, 2, chips)),
+            dma((ITERS, 2, chips)),
+            dma((ITERS, 2, chips)),
+            dma((ITERS, 2, chips)),
         ],
         compiler_params=pltpu.CompilerParams(
             collective_id=0, has_side_effects=True, vmem_limit_bytes=48 * 1024 * 1024
         ),
-    )(volume, measured, row_taps, col_taps, phase_map, radius)
+    )(*(
+        pltpu.with_memory_space_constraint(x, pltpu.HBM)
+        for x in (volume, measured, row_taps, jnp.transpose(col_taps, (1, 0, 2)), phase_map, radius)
+    ))
 
 
 def solution(mesh):

time: 71.9 us -> 65.6 us (0.912)
  local copies, waits for them, and re-layouts: 5.8 us -> 1.84 us
  Pallas kernels: 65.8 us -> 63.7 us
    unnamed x10 -> x1, local copies, waits for them, and re-layouts: 5.8 us -> 1.84 us
    pallas_call x1, Pallas kernels: 65.8 us -> 63.7 us  [local(): pl.pallas_call(functools.partial(kernel, depths, strips), out_shape=jax.S...]
where the time goes in v1:
time: 65.6 us; the launch traced here: 65.5 us
  Pallas kernels  63.7 us (97%)
  local copies, waits for them, and re-layouts  1.84 us (3%)
    pallas_call x1, Pallas kernels, local(): pl.pallas_call(functools.partial(kernel, depths, strips), out_shape=jax.S...  63.7 us
    unnamed x1, local copies, waits for them, and re-layouts  1.84 us

profile of v1, /device:TPU:1, one launch (start us, length us, event | category | flops | bytes accessed | tf_op | source)
XLA Modules:
  0.0 65.5 jit_solution(5732768417551604037)
XLA Ops:
  0.0 63.7 %shard_map.64 = f32[4,120,1920]{2,1,0:T(8,128)S(1)} custom-call(f32[4,120,1920]{2,1,0:T(8,128)} %vol_hbm.1, f32[120,1920]{1,0:T(8,128)} %meas_hbm.1, f32[4,31]{1,0:T(4,128)} %rt_hbm.1, f32[15,4,31]{2,1,0:T(4,128)} %bitcast.1, s32[4,15]{1,0:T(4,128)} %pm_hbm.1, s32[4]{0:T(128)} %rad_hbm.1), custom_call_target="tpu_custom_call" | custom-call | tf_op jit(solution)/shard_map/pallas_call | solution.py:378
  63.7 1.8 %copy.8 = f32[4,120,1920]{2,1,0:T(8,128)} copy(f32[4,120,1920]{2,1,0:T(8,128)S(1)} %shard_map.64) | data formatting | bytes 7372800

commit v2 on v1

v2 whole, which is shorter than its diff:
```python
import functools

import jax
import jax.numpy as jnp
from jax import lax
from jax.experimental import pallas as pl
from jax.experimental.pallas import tpu as pltpu
from jax.sharding import PartitionSpec as P

PITCH = 15
RMAX = 15
TAPS = 2 * RMAX + 1
ITERS = 2
LANE = 128
WIN = 256
BW = 225
FIRST = (0, 795)
SPREAD = (((0, 5), (1, 4)), ((0, 4), (0, 5)))
CHUNKS = (((0, 8), (8, 7)), ((0, 7), (7, 8)))
BACK = ((5, 5), (4, 5))
SPLIT = (1005, 870)
MOST = 5
HALO = 16
MESH = pl.DeviceIdType.MESH
BF = jnp.bfloat16
F32 = jnp.float32


def iota(shape, axis):
    return lax.broadcasted_iota(jnp.int32, shape, axis)


def dot(a, b):
    return jnp.dot(a, b, preferred_element_type=F32)


def unwindow(ref, k, rows, start):
    b0, l0 = divmod(LANE * k - start, BW)
    if b0 < 0:
        return pltpu.roll(ref[:rows, 0:LANE], start - LANE * k, axis=1)
    n0 = min(LANE, BW - l0)
    base = WIN * b0
    if l0 == 0:
        a = ref[:rows, base : base + LANE]
    elif l0 < LANE:
        a = pltpu.roll(ref[:rows, base : base + WIN], WIN - l0, axis=1)[:, :LANE]
    elif l0 == LANE:
        a = ref[:rows, base + LANE : base + WIN]
    else:
        a = pltpu.roll(ref[:rows, base + LANE : base + WIN], WIN - l0, axis=1)
    if n0 < LANE:
        b = pltpu.roll(ref[:rows, base + WIN : base + WIN + LANE], n0, axis=1)
        a = jnp.where(iota(a.shape, 1) < n0, a, b)
    return a


def kernel(depths, strips, vol_hbm, meas_hbm, rt_hbm, ct_hbm, pm_hbm, rad_hbm, out_hbm,
           rt_ref, ct_ref, pm_ref, rad_ref,
           v32, spr, pw, pc, sb, qb, rb, s_ref, hb, mc, rc, wr, ga, bpw,
           ctf, up, fm, gm, bt, bfm, cinv, rinv,
           sem_vol, sem_out, sem_in, sem_ms, sem_mr, sem_ps, sem_pr, sem_rs, sem_rr,
           sem_hs, sem_hr, sem_as, sem_ar, sem_fs, sem_fr):
    planes, rows, cols = vol_hbm.shape
    ext = rows + 2 * HALO
    kext = ga.shape[0]
    edge = 4 * HALO
    nk = cols // LANE
    chips = depths // 2
    d = lax.axis_index("depth")
    s = lax.axis_index("strip")
    c = lax.rem(d, 2)
    chip = d // 2
    sibling = d + 1 - 2 * c
    above = lax.rem(s + strips - 1, strips)
    below = lax.rem(s + 1, strips)
    peers = [lax.rem(chip + r, chips) for r in range(chips)]
    givers = [lax.rem(chip + chips - r, chips) for r in range(chips)]

    def strip_row(p):
        return jnp.where(p < 2 * HALO, p + rows - HALO, p - 3 * HALO)

    arg_in = []
    for i, (src, dst) in enumerate(
        ((rt_hbm, rt_ref), (ct_hbm, ct_ref), (pm_hbm, pm_ref), (rad_hbm, rad_ref))
    ):
        copy = pltpu.make_async_copy(src, dst, sem_in.at[i])
        copy.start()
        arg_in.append(copy)
    vol_in = []
    for z in range(planes):
        copy = pltpu.make_async_copy(
            vol_hbm.at[z], v32.at[z, 0:rows, LANE : LANE + cols], sem_vol.at[z]
        )
        copy.start()
        vol_in.append(copy)
    mc_in = []
    for it in range(ITERS):
        mine = CHUNKS[it][0][0] + (CHUNKS[it][1][0] - CHUNKS[it][0][0]) * c + chip
        col0 = pl.multiple_of(jnp.minimum(mine, nk - 1) * LANE, LANE)
        mc_in.append(pltpu.make_async_copy(
            meas_hbm.at[0 : rows - HALO, pl.ds(col0, LANE)],
            mc.at[it, 3 * HALO : ext, :], sem_in.at[4 + 2 * it],
        ))
        mc_in.append(pltpu.make_async_copy(
            meas_hbm.at[rows - HALO : rows, pl.ds(col0, LANE)],
            mc.at[it, 0:HALO, :], sem_in.at[5 + 2 * it],
        ))
    for copy in mc_in:
        copy.start()

    barrier = pltpu.get_barrier_semaphore()
    pl.semaphore_signal(barrier, inc=1, device_id={"depth": sibling}, device_id_type=MESH)
    for r in range(1, chips):
        pl.semaphore_signal(
            barrier, inc=1, device_id={"depth": 2 * peers[r] + c}, device_id_type=MESH
        )
    for t in (above, below):
        pl.semaphore_signal(barrier, inc=1, device_id={"strip": t}, device_id_type=MESH)

    for z in range(planes):
        v32[z, rows:, :] = jnp.zeros((LANE - rows, v32.shape[2]), F32)
        v32[z, :, 0:LANE] = jnp.zeros((LANE, LANE), F32)
        v32[z, :, LANE + cols :] = jnp.zeros((LANE, v32.shape[2] - LANE - cols), F32)
    for it in range(ITERS):
        for q in range(2):
            for k in range(CHUNKS[it][q][1], chips):
                pc[it, q, k] = jnp.zeros((ext, LANE), BF)
        rc[it, 0] = jnp.zeros((kext, LANE), BF)
        rc[it, nk + 1] = jnp.zeros((kext, LANE), BF)
        for k in range(1, nk + 1):
            rc[it, k, ext:, :] = jnp.zeros((kext - ext, LANE), BF)

    up[...] = jnp.zeros_like(up)
    every = jnp.where(lax.rem(iota((WIN, LANE), 0), PITCH) == iota((WIN, LANE), 1), 1.0, 0.0)
    every = every.astype(BF)
    y = s * rows + strip_row(iota((kext, LANE), 0))
    inside = (y >= 0) & (y < rows * strips) & (iota((kext, LANE), 0) < ext)
    inside = jnp.where(inside, 1.0, 0.0).astype(BF)
    block = iota((16, WIN), 0)
    xo = jnp.where(block < MOST, FIRST[0] + BW * block, FIRST[1] + BW * (block - MOST))
    xo = xo + iota((16, WIN), 1)
    xs = xo - RMAX
    ones_win = jnp.where((xs >= 0) & (xs < cols), 1.0, 0.0).astype(BF)
    col_ok = (xo < cols) & (iota((16, WIN), 1) < BW)
    row_ok = iota((LANE, LANE), 0) < rows
    for copy in arg_in:
        copy.wait()
    for z in range(planes):
        reach = rad_ref[z]
        ctf[...] = jnp.zeros_like(ctf)
        keep = jnp.abs(iota((PITCH, TAPS), 1) - RMAX) <= reach
        ctf[0:PITCH, 0:TAPS] = jnp.where(keep, ct_ref[:, z, :], 0.0)
        keep1 = jnp.abs(iota((1, TAPS), 1) - RMAX) <= reach
        ctf[16:17, 0:TAPS] = jnp.where(keep1, rt_ref[z : z + 1, :], 0.0)
        family = jnp.full((16, LANE), -1, jnp.int32)
        for p in range(PITCH):
            family = jnp.where(iota((16, LANE), 0) == p, pm_ref[z, p], family)
        pick = jnp.where(family == iota((16, LANE), 1), 1.0, 0.0).astype(BF)
        table = ctf[...].astype(BF)
        up[0:16, :] = dot(pick, table)
        taps = dot(every, up[...].astype(BF))
        taps = jnp.concatenate([taps, jnp.zeros((WIN, WIN - LANE), F32)], axis=1)
        fwd = pltpu.roll(taps, 32 - 2 * RMAX, axis=1)
        fwd = pltpu.roll(fwd, WIN - 32, axis=1, stride=1, stride_axis=0)
        fm[z] = fwd.astype(BF)
        back = pltpu.roll(taps, 0, axis=1, stride=1, stride_axis=0)
        gm[z] = jnp.transpose(back).astype(BF)
        rtap = jnp.concatenate([ctf[16:17, :], jnp.zeros((1, WIN - LANE), F32)], axis=1)
        rtap = jnp.broadcast_to(rtap, (LANE, WIN))
        band = pltpu.roll(rtap, 1, axis=1)
        band = pltpu.roll(band, 0, axis=1, stride=1, stride_axis=0)
        p = iota((LANE, WIN), 1)
        last = pltpu.roll(band, WIN - rows, axis=1)
        band = jnp.where(p < 2 * HALO, last, pltpu.roll(band, 2 * HALO, axis=1))
        band = jnp.where(p < ext, band, 0.0)
        bt[z] = band[:, :kext].astype(BF)
        bfm[:, LANE * z : LANE * (z + 1)] = jnp.transpose(band)[:kext, :].astype(BF)
        rn = dot(bt[z], inside)
        rinv[z] = jnp.where(row_ok, 1.0 / rn, 0.0)
        cn = dot(ones_win, gm[z])
        cinv[z] = jnp.where(col_ok, 1.0 / cn, 0.0)

    pl.semaphore_wait(barrier, chips + 2)
    for copy in mc_in:
        copy.wait()
    def m_up(it):
        return pltpu.make_async_remote_copy(
            src_ref=mc.at[it, 3 * HALO : 4 * HALO, :], dst_ref=mc.at[it, HALO : 2 * HALO, :],
            send_sem=sem_ms.at[it, 0], recv_sem=sem_mr.at[it, 0],
            device_id={"strip": above}, device_id_type=MESH,
        )

    def m_down(it):
        return pltpu.make_async_remote_copy(
            src_ref=mc.at[it, 0:HALO, :], dst_ref=mc.at[it, 2 * HALO : 3 * HALO, :],
            send_sem=sem_ms.at[it, 1], recv_sem=sem_mr.at[it, 1],
            device_id={"strip": below}, device_id_type=MESH,
        )

    for it in range(ITERS):
        m_up(it).start()
        m_down(it).start()
    for copy in vol_in:
        copy.wait()

    def groups(count):
        return [(g, min(3, count - g)) for g in range(0, count, 3)]

    def window(z, start):
        q, sh = divmod(LANE - RMAX + start, LANE)
        x = v32[z, :, LANE * q : LANE * q + WIN + LANE]
        if sh:
            x = pltpu.roll(x, WIN + LANE - sh, axis=1)
        return x[:, :WIN].astype(BF)

    def spread(it, q):
        first, count = SPREAD[it][q]
        start = FIRST[q] + BW * first

        @pl.loop(0, planes)
        def _(z):
            for g, n in groups(count):
                lhs = jnp.concatenate([window(z, start + BW * (g + i)) for i in range(n)], axis=0)
                res = dot(lhs, fm[z])
                for i in range(n):
                    spr[pl.ds(pl.multiple_of(z * LANE, LANE), LANE),
                        WIN * (g + i) : WIN * (g + i + 1)] = (
                        res[LANE * i : LANE * (i + 1)].astype(BF)
                    )

    def sensor_part(it, q):
        first, count = SPREAD[it][q]
        start = FIRST[q] + BW * first
        for b in range(count):
            pw[:, WIN * b : WIN * (b + 1)] = dot(bfm[...], spr[:, WIN * b : WIN * (b + 1)])
        base, n = CHUNKS[it][q]
        for k in range(n):
            pc[it, q, k] = unwindow(pw, base + k, ext, start).astype(BF)

    def pair(it, q):
        return pltpu.make_async_remote_copy(
            src_ref=pc.at[it, q], dst_ref=sb.at[it],
            send_sem=sem_ps.at[it], recv_sem=sem_pr.at[it],
            device_id={"depth": sibling}, device_id_type=MESH,
        )

    def part(it, r):
        return pltpu.make_async_remote_copy(
            src_ref=qb.at[it, r], dst_ref=rb.at[it, r],
            send_sem=sem_rs.at[it, r], recv_sem=sem_rr.at[it, r],
            device_id={"depth": 2 * peers[r] + c}, device_id_type=MESH,
        )

    def h_up(it):
        return pltpu.make_async_remote_copy(
            src_ref=s_ref.at[it, 2 * HALO : edge], dst_ref=hb.at[it, 0 : 2 * HALO],
            send_sem=sem_hs.at[it, 0], recv_sem=sem_hr.at[it, 0],
            device_id={"strip": above}, device_id_type=MESH,
        )

    def h_down(it):
        return pltpu.make_async_remote_copy(
            src_ref=s_ref.at[it, 0 : 2 * HALO], dst_ref=hb.at[it, 2 * HALO : edge],
            send_sem=sem_hs.at[it, 1], recv_sem=sem_hr.at[it, 1],
            device_id={"strip": below}, device_id_type=MESH,
        )

    def slot(it, q, k):
        base, n = CHUNKS[it][q]
        if n == chips:
            return 1 + base + k
        return 1 + base + k + (k // n) * (nk + 1 - base - n)

    def give(it, at, target, send, recv):
        at = rc.at[it, at, 0:ext, :]
        return pltpu.make_async_remote_copy(
            src_ref=at, dst_ref=at, send_sem=send, recv_sem=recv,
            device_id={"depth": target}, device_id_type=MESH,
        )

    def to_chip(it, q, r):
        return give(it, slot(it, q, chip), 2 * peers[r] + c, sem_as.at[it, r], sem_ar.at[it, r])

    def from_chip(it, q, r):
        return give(it, slot(it, q, givers[r]), sibling, sem_as.at[it, r], sem_ar.at[it, r])

    def to_core(it, q, r):
        return give(it, slot(it, q, givers[r]), sibling, sem_fs.at[it, r], sem_fr.at[it, r])

    def pair_send(it, q):
        @pl.when(c != q)
        def _():
            pair(it, q).start()

    def part_send(it, q):
        @pl.when(c == q)
        def _():
            pair(it, q).wait_recv()
            for r in range(1, chips):
                k = peers[r]
                qb[it, r] = (pc[it, q, k].astype(F32) + sb[it, k].astype(F32)).astype(BF)
                part(it, r).start()

    def ratio_send(it, q):
        @pl.when(c == q)
        def _():
            total = pc[it, q, chip].astype(F32) + sb[it, chip].astype(F32)
            for r in range(1, chips):
                part(it, r).wait_recv()
                total = total + rb[it, r].astype(F32)
            s_ref[it] = total
            h_up(it).start()
            h_down(it).start()
            m_up(it).wait_recv()
            m_down(it).wait_recv()
            y = s * rows + strip_row(iota((ext, LANE), 0))
            ok = (y >= 0) & (y < rows * strips) & (chip < CHUNKS[it][q][1])
            mine = slot(it, q, chip)
            ratio = jnp.where(ok[edge:], mc[it, edge:, :] / s_ref[it, edge:, :], 0.0)
            rc[it, mine, edge:ext, :] = ratio.astype(BF)
            h_up(it).wait_recv()
            h_down(it).wait_recv()
            first = iota((edge, LANE), 0) < 2 * HALO
            other = (first & (s < strips - 1)) | (~first & (s > 0))
            shared = s_ref[it, 0:edge, :] + jnp.where(other, hb[it], 0.0)
            ratio = jnp.where(ok[:edge], mc[it, 0:edge, :] / shared, 0.0)
            rc[it, mine, 0:edge, :] = ratio.astype(BF)
            for r in range(1, chips):
                to_chip(it, q, r).start()
            to_core(it, q, 0).start()

    def ratio_forward(it, q):
        @pl.when(c == q)
        def _():
            for r in range(1, chips):
                from_chip(it, q, r).wait_recv()
                to_core(it, q, r).start()

    def ratio_arrived(it, q):
        @pl.when(c != q)
        def _():
            for r in range(chips):
                to_core(it, q, r).wait_recv()

    def back(it, q):
        count = BACK[it][q]
        last = CHUNKS[it][q][0] + CHUNKS[it][q][1]
        for b in range(count):
            at, sh = divmod(LANE - RMAX + FIRST[q] + BW * b, LANE)
            pieces = [
                rc[it, at + i].astype(F32)
                if at + i <= last or q == 1 else jnp.zeros((kext, LANE), F32)
                for i in range(3)
            ]
            x = jnp.concatenate(pieces, axis=1)
            if sh:
                x = pltpu.roll(x, WIN + LANE - sh, axis=1)
            wr[kext * b : kext * (b + 1), :] = x[:, :WIN].astype(BF)
        lo = SPLIT[it] if q == 1 else 0
        hi = SPLIT[it] if q == 0 else cols

        @pl.loop(0, planes)
        def _(z):
            for g, n in groups(count):
                res = dot(wr[kext * g : kext * (g + n), :], gm[z])
                for i in range(n):
                    ga[:, WIN * (g + i) : WIN * (g + i + 1)] = (
                        res[kext * i : kext * (i + 1)].astype(BF)
                    )
            scale = jnp.concatenate([rinv[z], rinv[z]], axis=1)
            for b in range(count):
                bp = dot(bt[z], ga[:, WIN * b : WIN * (b + 1)])
                row = MOST * q + b
                bpw[:, WIN * b : WIN * (b + 1)] = bp * scale * cinv[z, row : row + 1, :]
            for k in range(lo // LANE, -(-hi // LANE)):
                at = slice(LANE * (k + 1), LANE * (k + 2))
                factor = unwindow(bpw, k, LANE, FIRST[q])
                x = iota(factor.shape, 1) + LANE * k
                if LANE * k < lo:
                    factor = jnp.where(x >= lo, factor, 1.0)
                if LANE * (k + 1) > hi:
                    factor = jnp.where(x < hi, factor, 1.0)
                v32[z, :, at] = v32[z, :, at] * factor
            if it == ITERS - 1 and q == 1:
                pltpu.make_async_copy(
                    v32.at[z, 0:rows, LANE : LANE + cols], out_hbm.at[z], sem_out.at[z]
                ).start()

    def forward(it, q):
        spread(it, q)
        if it == 0 and q == 1:
            part_send(it, 0)
        sensor_part(it, q)
        pair_send(it, q)
        if it > 0 or q == 1:
            part_send(it, q)

    forward(0, 0)
    forward(0, 1)
    for it in range(ITERS):
        ratio_send(it, 0)
        ratio_send(it, 1)
        ratio_forward(it, 0)
        ratio_arrived(it, 0)
        back(it, 0)
        ratio_forward(it, 1)
        if it + 1 < ITERS:
            forward(it + 1, 0)
        ratio_arrived(it, 1)
        back(it, 1)
        if it + 1 < ITERS:
            forward(it + 1, 1)

    for it in range(ITERS):
        m_up(it).wait_send()
        m_down(it).wait_send()
        for q in range(2):
            @pl.when(c != q)
            def _():
                pair(it, q).wait_send()

            @pl.when(c == q)
            def _():
                h_up(it).wait_send()
                h_down(it).wait_send()
                for r in range(1, chips):
                    part(it, r).wait_send()
                    to_chip(it, q, r).wait_send()
                for r in range(chips):
                    to_core(it, q, r).wait_send()
    for z in range(planes):
        pltpu.make_async_copy(
            v32.at[z, 0:rows, LANE : LANE + cols], out_hbm.at[z], sem_out.at[z]
        ).wait()


def local(depths, strips, volume, measured, row_taps, col_taps, phase_map, radius):
    planes, rows, cols = volume.shape
    ext = rows + 2 * HALO
    kext = 160
    nk = cols // LANE
    chips = depths // 2
    dma = pltpu.SemaphoreType.DMA
    vmem = pltpu.VMEM
    return pl.pallas_call(
        functools.partial(kernel, depths, strips),
        out_shape=jax.ShapeDtypeStruct(volume.shape, F32),
        in_specs=[pl.BlockSpec(memory_space=pltpu.HBM)] * 6,
        out_specs=pl.BlockSpec(memory_space=pl.ANY),
        scratch_shapes=[
            vmem(row_taps.shape, F32),
            vmem((PITCH, planes, TAPS), F32),
            pltpu.SMEM(phase_map.shape, jnp.int32),
            pltpu.SMEM(radius.shape, jnp.int32),
            vmem((planes, LANE, cols + 2 * LANE), F32),
            vmem((planes * LANE, MOST * WIN), BF),
            vmem((kext, MOST * WIN), F32),
            vmem((ITERS, 2, chips, ext, LANE), BF),
            vmem((ITERS, chips, ext, LANE), BF),
            vmem((ITERS, chips, ext, LANE), BF),
            vmem((ITERS, chips, ext, LANE), BF),
            vmem((ITERS, ext, LANE), F32),
            vmem((ITERS, 4 * HALO, LANE), F32),
            vmem((ITERS, ext, LANE), F32),
            vmem((ITERS, nk + 3, kext, LANE), BF),
            vmem((MOST * kext, WIN), BF),
            vmem((kext, MOST * WIN), BF),
            vmem((LANE, MOST * WIN), F32),
            vmem((LANE, LANE), F32),
            vmem((LANE, LANE), F32),
            vmem((planes, WIN, WIN), BF),
            vmem((planes, WIN, WIN), BF),
            vmem((planes, LANE, kext), BF),
            vmem((kext, planes * LANE), BF),
            vmem((planes, 16, WIN), F32),
            vmem((planes, LANE, LANE), F32),
            dma((planes,)),
            dma((planes,)),
            dma((4 + 2 * ITERS,)),
            dma((ITERS, 2)),
            dma((ITERS, 2)),
            dma((ITERS,)),
            dma((ITERS,)),
            dma((ITERS, chips)),
            dma((ITERS, chips)),
            dma((ITERS, 2)),
            dma((ITERS, 2)),
            dma((ITERS, chips)),
            dma((ITERS, chips)),
            dma((ITERS, chips)),
            dma((ITERS, chips)),
        ],
        compiler_params=pltpu.CompilerParams(
            collective_id=0, has_side_effects=True, vmem_limit_bytes=48 * 1024 * 1024
        ),
    )(*(
        pltpu.with_memory_space_constraint(x, pltpu.HBM)
        for x in (volume, measured, row_taps, jnp.transpose(col_taps, (1, 0, 2)), phase_map, radius)
    ))


def solution(mesh):
    return jax.shard_map(
        functools.partial(local, mesh.shape["depth"], mesh.shape["strip"]),
        mesh=mesh,
        in_specs=(
            P("depth", "strip", None),
            P("strip", None),
            P("depth", None),
            P("depth", None, None),
            P("depth", None),
            P("depth"),
        ),
        out_specs=P("depth", "strip", None),
        check_vma=False,
    )
```

time: 65.6 us -> 63 us (0.960)
  Pallas kernels: 63.7 us -> 61 us
    pallas_call x1, Pallas kernels: 63.7 us -> 61 us  [local(): pl.pallas_call(functools.partial(kernel, depths, strips), out_shape=jax.S...]
where the time goes in v2:
time: 63 us; the launch traced here: 62.9 us
  Pallas kernels  61 us (97%)
  local copies, waits for them, and re-layouts  1.84 us (3%)
    pallas_call x1, Pallas kernels, local(): pl.pallas_call(functools.partial(kernel, depths, strips), out_shape=jax.S...  61 us
    unnamed x1, local copies, waits for them, and re-layouts  1.84 us

profile of v2, /device:TPU:1, one launch (start us, length us, event | category | flops | bytes accessed | tf_op | source)
XLA Modules:
  0.0 62.9 jit_solution(1911716281048113947)
XLA Ops:
  0.0 61.0 %shard_map.64 = f32[4,120,1920]{2,1,0:T(8,128)S(1)} custom-call(f32[4,120,1920]{2,1,0:T(8,128)} %vol_hbm.1, f32[120,1920]{1,0:T(8,128)} %meas_hbm.1, f32[4,31]{1,0:T(4,128)} %rt_hbm.1, f32[15,4,31]{2,1,0:T(4,128)} %bitcast.1, s32[4,15]{1,0:T(4,128)} %pm_hbm.1, s32[4]{0:T(128)} %rad_hbm.1), custom_call_target="tpu_custom_call" | custom-call | tf_op jit(solution)/shard_map/pallas_call | solution.py:445
  61.0 1.8 %copy.8 = f32[4,120,1920]{2,1,0:T(8,128)} copy(f32[4,120,1920]{2,1,0:T(8,128)S(1)} %shard_map.64) | data formatting | bytes 7372800

commit v3 on v2

--- a/solution.py
+++ b/solution.py
@@ -56,13 +56,13 @@
 
 def kernel(depths, strips, vol_hbm, meas_hbm, rt_hbm, ct_hbm, pm_hbm, rad_hbm, out_hbm,
            rt_ref, ct_ref, pm_ref, rad_ref,
-           v32, spr, pw, pc, sb, qb, rb, s_ref, hb, mc, rc, wr, ga, bpw,
+           v32, spr, pw, pc, sb, qb, rb, ub, mc, rc, wr, ga, bpw,
            ctf, up, fm, gm, bt, bfm, cinv, rinv,
            sem_vol, sem_out, sem_in, sem_ms, sem_mr, sem_ps, sem_pr, sem_rs, sem_rr,
            sem_hs, sem_hr, sem_as, sem_ar, sem_fs, sem_fr):
     planes, rows, cols = vol_hbm.shape
     ext = rows + 2 * HALO
-    kext = ga.shape[0]
+    kext = ga.shape[1]
     edge = 4 * HALO
     nk = cols // LANE
     chips = depths // 2
@@ -73,8 +73,12 @@
     sibling = d + 1 - 2 * c
     above = lax.rem(s + strips - 1, strips)
     below = lax.rem(s + 1, strips)
-    peers = [lax.rem(chip + r, chips) for r in range(chips)]
-    givers = [lax.rem(chip + chips - r, chips) for r in range(chips)]
+    ys = chips // 2
+    xc, yc = chip // ys, lax.rem(chip, ys)
+    peers = [lax.rem(xc + r // ys, 2) * ys + lax.rem(yc + r, ys) for r in range(chips)]
+    givers = [lax.rem(xc + r // ys, 2) * ys + lax.rem(yc + ys - r % ys, ys) for r in range(chips)]
+    near = sorted(range(1, chips), key=lambda r: 2 * (r // ys) + min(r % ys, ys - r % ys))
+    far = near[::-1]
 
     def strip_row(p):
         return jnp.where(p < 2 * HALO, p + rows - HALO, p - 3 * HALO)
@@ -115,7 +119,11 @@
             barrier, inc=1, device_id={"depth": 2 * peers[r] + c}, device_id_type=MESH
         )
     for t in (above, below):
-        pl.semaphore_signal(barrier, inc=1, device_id={"strip": t}, device_id_type=MESH)
+        for r in range(chips):
+            pl.semaphore_signal(
+                barrier, inc=1, device_id={"depth": 2 * peers[r] + c, "strip": t},
+                device_id_type=MESH,
+            )
 
     for z in range(planes):
         v32[z, rows:, :] = jnp.zeros((LANE - rows, v32.shape[2]), F32)
@@ -180,7 +188,7 @@
         cn = dot(ones_win, gm[z])
         cinv[z] = jnp.where(col_ok, 1.0 / cn, 0.0)
 
-    pl.semaphore_wait(barrier, chips + 2)
+    pl.semaphore_wait(barrier, 3 * chips)
     for copy in mc_in:
         copy.wait()
     def m_up(it):
@@ -217,13 +225,12 @@
         first, count = SPREAD[it][q]
         start = FIRST[q] + BW * first
 
-        @pl.loop(0, planes)
-        def _(z):
+        for z in range(planes):
             for g, n in groups(count):
                 lhs = jnp.concatenate([window(z, start + BW * (g + i)) for i in range(n)], axis=0)
                 res = dot(lhs, fm[z])
                 for i in range(n):
-                    spr[pl.ds(pl.multiple_of(z * LANE, LANE), LANE),
+                    spr[z * LANE : (z + 1) * LANE,
                         WIN * (g + i) : WIN * (g + i + 1)] = (
                         res[LANE * i : LANE * (i + 1)].astype(BF)
                     )
@@ -251,18 +258,20 @@
             device_id={"depth": 2 * peers[r] + c}, device_id_type=MESH,
         )
 
-    def h_up(it):
-        return pltpu.make_async_remote_copy(
-            src_ref=s_ref.at[it, 2 * HALO : edge], dst_ref=hb.at[it, 0 : 2 * HALO],
-            send_sem=sem_hs.at[it, 0], recv_sem=sem_hr.at[it, 0],
-            device_id={"strip": above}, device_id_type=MESH,
-        )
-
-    def h_down(it):
-        return pltpu.make_async_remote_copy(
-            src_ref=s_ref.at[it, 0 : 2 * HALO], dst_ref=hb.at[it, 2 * HALO : edge],
-            send_sem=sem_hs.at[it, 1], recv_sem=sem_hr.at[it, 1],
-            device_id={"strip": below}, device_id_type=MESH,
+    def shared_part(it, side, r):
+        at = slice(2 * HALO, edge) if side == 0 else slice(0, 2 * HALO)
+        return pltpu.make_async_remote_copy(
+            src_ref=qb.at[it, r, at, :], dst_ref=ub.at[it, side, r],
+            send_sem=sem_hs.at[it, side], recv_sem=sem_hr.at[it, side],
+            device_id={"depth": 2 * peers[r] + c, "strip": (above, below)[side]},
+            device_id_type=MESH,
+        )
+
+    def all_shared(it, side):
+        return pltpu.make_async_remote_copy(
+            src_ref=ub.at[it, side], dst_ref=ub.at[it, side],
+            send_sem=sem_hs.at[it, side], recv_sem=sem_hr.at[it, side],
+            device_id={"strip": (above, below)[side]}, device_id_type=MESH,
         )
 
     def slot(it, q, k):
@@ -296,43 +305,45 @@
         @pl.when(c == q)
         def _():
             pair(it, q).wait_recv()
-            for r in range(1, chips):
+            for r in far + [0]:
                 k = peers[r]
                 qb[it, r] = (pc[it, q, k].astype(F32) + sb[it, k].astype(F32)).astype(BF)
-                part(it, r).start()
+                shared_part(it, 0, r).start()
+                shared_part(it, 1, r).start()
+                if r:
+                    part(it, r).start()
 
     def ratio_send(it, q):
         @pl.when(c == q)
         def _():
             total = pc[it, q, chip].astype(F32) + sb[it, chip].astype(F32)
-            for r in range(1, chips):
+            for r in near:
                 part(it, r).wait_recv()
                 total = total + rb[it, r].astype(F32)
-            s_ref[it] = total
-            h_up(it).start()
-            h_down(it).start()
             m_up(it).wait_recv()
             m_down(it).wait_recv()
+            all_shared(it, 0).wait_recv()
+            all_shared(it, 1).wait_recv()
+            shared = [ub[it, side, 0].astype(F32) for side in range(2)]
+            for r in range(1, chips):
+                shared = [shared[side] + ub[it, side, r].astype(F32) for side in range(2)]
+            total = jnp.concatenate([
+                total[0 : 2 * HALO] + jnp.where(s < strips - 1, shared[0], 0.0),
+                total[2 * HALO : edge] + jnp.where(s > 0, shared[1], 0.0),
+                total[edge:],
+            ], axis=0)
             y = s * rows + strip_row(iota((ext, LANE), 0))
             ok = (y >= 0) & (y < rows * strips) & (chip < CHUNKS[it][q][1])
             mine = slot(it, q, chip)
-            ratio = jnp.where(ok[edge:], mc[it, edge:, :] / s_ref[it, edge:, :], 0.0)
-            rc[it, mine, edge:ext, :] = ratio.astype(BF)
-            h_up(it).wait_recv()
-            h_down(it).wait_recv()
-            first = iota((edge, LANE), 0) < 2 * HALO
-            other = (first & (s < strips - 1)) | (~first & (s > 0))
-            shared = s_ref[it, 0:edge, :] + jnp.where(other, hb[it], 0.0)
-            ratio = jnp.where(ok[:edge], mc[it, 0:edge, :] / shared, 0.0)
-            rc[it, mine, 0:edge, :] = ratio.astype(BF)
-            for r in range(1, chips):
+            rc[it, mine, 0:ext, :] = jnp.where(ok, mc[it] / total, 0.0).astype(BF)
+            for r in far:
                 to_chip(it, q, r).start()
             to_core(it, q, 0).start()
 
     def ratio_forward(it, q):
         @pl.when(c == q)
         def _():
-            for r in range(1, chips):
+            for r in near:
                 from_chip(it, q, r).wait_recv()
                 to_core(it, q, r).start()
 
@@ -359,22 +370,21 @@
         lo = SPLIT[it] if q == 1 else 0
         hi = SPLIT[it] if q == 0 else cols
 
-        @pl.loop(0, planes)
-        def _(z):
+        for z in range(planes):
             for g, n in groups(count):
                 res = dot(wr[kext * g : kext * (g + n), :], gm[z])
                 for i in range(n):
-                    ga[:, WIN * (g + i) : WIN * (g + i + 1)] = (
+                    ga[z % 2, :, WIN * (g + i) : WIN * (g + i + 1)] = (
                         res[kext * i : kext * (i + 1)].astype(BF)
                     )
             scale = jnp.concatenate([rinv[z], rinv[z]], axis=1)
             for b in range(count):
-                bp = dot(bt[z], ga[:, WIN * b : WIN * (b + 1)])
+                bp = dot(bt[z], ga[z % 2, :, WIN * b : WIN * (b + 1)])
                 row = MOST * q + b
-                bpw[:, WIN * b : WIN * (b + 1)] = bp * scale * cinv[z, row : row + 1, :]
+                bpw[z % 2, :, WIN * b : WIN * (b + 1)] = bp * scale * cinv[z, row : row + 1, :]
             for k in range(lo // LANE, -(-hi // LANE)):
                 at = slice(LANE * (k + 1), LANE * (k + 2))
-                factor = unwindow(bpw, k, LANE, FIRST[q])
+                factor = unwindow(bpw.at[z % 2], k, LANE, FIRST[q])
                 x = iota(factor.shape, 1) + LANE * k
                 if LANE * k < lo:
                     factor = jnp.where(x >= lo, factor, 1.0)
@@ -421,8 +431,8 @@
 
             @pl.when(c == q)
             def _():
-                h_up(it).wait_send()
-                h_down(it).wait_send()
+                all_shared(it, 0).wait_send()
+                all_shared(it, 1).wait_send()
                 for r in range(1, chips):
                     part(it, r).wait_send()
                     to_chip(it, q, r).wait_send()
@@ -459,13 +469,12 @@
             vmem((ITERS, chips, ext, LANE), BF),
             vmem((ITERS, chips, ext, LANE), BF),
             vmem((ITERS, chips, ext, LANE), BF),
-            vmem((ITERS, ext, LANE), F32),
-            vmem((ITERS, 4 * HALO, LANE), F32),
+            vmem((ITERS, 2, chips, 2 * HALO, LANE), BF),
             vmem((ITERS, ext, LANE), F32),
             vmem((ITERS, nk + 3, kext, LANE), BF),
             vmem((MOST * kext, WIN), BF),
-            vmem((kext, MOST * WIN), BF),
-            vmem((LANE, MOST * WIN), F32),
+            vmem((2, kext, MOST * WIN), BF),
+            vmem((2, LANE, MOST * WIN), F32),
             vmem((LANE, LANE), F32),
             vmem((LANE, LANE), F32),
             vmem((planes, WIN, WIN), BF),

time: 63 us -> 52.7 us (0.84)
  Pallas kernels: 61 us -> 50.8 us
    pallas_call x1, Pallas kernels: 61 us -> 50.8 us  [local(): pl.pallas_call(functools.partial(kernel, depths, strips), out_shape=jax.S...]
where the time goes in v3:
time: 52.7 us; the launch traced here: 52.6 us
  Pallas kernels  50.8 us (96%)
  local copies, waits for them, and re-layouts  1.84 us (3%)
    pallas_call x1, Pallas kernels, local(): pl.pallas_call(functools.partial(kernel, depths, strips), out_shape=jax.S...  50.8 us
    unnamed x1, local copies, waits for them, and re-layouts  1.84 us

profile of v3, /device:TPU:1, one launch (start us, length us, event | category | flops | bytes accessed | tf_op | source)
XLA Modules:
  0.0 52.6 jit_solution(4573646801925712652)
XLA Ops:
  0.0 50.8 %shard_map.64 = f32[4,120,1920]{2,1,0:T(8,128)S(1)} custom-call(f32[4,120,1920]{2,1,0:T(8,128)} %vol_hbm.1, f32[120,1920]{1,0:T(8,128)} %meas_hbm.1, f32[4,31]{1,0:T(4,128)} %rt_hbm.1, f32[15,4,31]{2,1,0:T(4,128)} %bitcast.1, s32[4,15]{1,0:T(4,128)} %pm_hbm.1, s32[4]{0:T(128)} %rad_hbm.1), custom_call_target="tpu_custom_call" | custom-call | tf_op jit(solution)/shard_map/pallas_call | solution.py:455
  50.8 1.8 %copy.8 = f32[4,120,1920]{2,1,0:T(8,128)} copy(f32[4,120,1920]{2,1,0:T(8,128)S(1)} %shard_map.64) | data formatting | bytes 7372800

commit v4 on v3

--- a/solution.py
+++ b/solution.py
@@ -57,7 +57,7 @@
 def kernel(depths, strips, vol_hbm, meas_hbm, rt_hbm, ct_hbm, pm_hbm, rad_hbm, out_hbm,
            rt_ref, ct_ref, pm_ref, rad_ref,
            v32, spr, pw, pc, sb, qb, rb, ub, mc, rc, wr, ga, bpw,
-           ctf, up, fm, gm, bt, bfm, cinv, rinv,
+           ctf, up, tap_ref, fm, gm, bt, bfm, cinv, rinv,
            sem_vol, sem_out, sem_in, sem_ms, sem_mr, sem_ps, sem_pr, sem_rs, sem_rr,
            sem_hs, sem_hr, sem_as, sem_ar, sem_fs, sem_fr):
     planes, rows, cols = vol_hbm.shape
@@ -80,6 +80,19 @@
     near = sorted(range(1, chips), key=lambda r: 2 * (r // ys) + min(r % ys, ys - r % ys))
     far = near[::-1]
 
+    barrier = pltpu.get_barrier_semaphore()
+    pl.semaphore_signal(barrier, inc=1, device_id={"depth": sibling}, device_id_type=MESH)
+    for r in range(1, chips):
+        pl.semaphore_signal(
+            barrier, inc=1, device_id={"depth": 2 * peers[r] + c}, device_id_type=MESH
+        )
+    for t in (above, below):
+        for r in range(chips):
+            pl.semaphore_signal(
+                barrier, inc=1, device_id={"depth": 2 * peers[r] + c, "strip": t},
+                device_id_type=MESH,
+            )
+
     def strip_row(p):
         return jnp.where(p < 2 * HALO, p + rows - HALO, p - 3 * HALO)
 
@@ -90,13 +103,18 @@
         copy = pltpu.make_async_copy(src, dst, sem_in.at[i])
         copy.start()
         arg_in.append(copy)
-    vol_in = []
+    def vol_in(z):
+        return pltpu.make_async_copy(
+            vol_hbm.at[z], v32.at[z, 0:rows, LANE : LANE + cols], sem_vol.at[z]
+        )
+
+    def vol_out(z):
+        return pltpu.make_async_copy(
+            v32.at[z, 0:rows, LANE : LANE + cols], out_hbm.at[z], sem_out.at[z]
+        )
+
     for z in range(planes):
-        copy = pltpu.make_async_copy(
-            vol_hbm.at[z], v32.at[z, 0:rows, LANE : LANE + cols], sem_vol.at[z]
-        )
-        copy.start()
-        vol_in.append(copy)
+        vol_in(z).start()
     mc_in = []
     for it in range(ITERS):
         mine = CHUNKS[it][0][0] + (CHUNKS[it][1][0] - CHUNKS[it][0][0]) * c + chip
@@ -112,19 +130,6 @@
     for copy in mc_in:
         copy.start()
 
-    barrier = pltpu.get_barrier_semaphore()
-    pl.semaphore_signal(barrier, inc=1, device_id={"depth": sibling}, device_id_type=MESH)
-    for r in range(1, chips):
-        pl.semaphore_signal(
-            barrier, inc=1, device_id={"depth": 2 * peers[r] + c}, device_id_type=MESH
-        )
-    for t in (above, below):
-        for r in range(chips):
-            pl.semaphore_signal(
-                barrier, inc=1, device_id={"depth": 2 * peers[r] + c, "strip": t},
-                device_id_type=MESH,
-            )
-
     for z in range(planes):
         v32[z, rows:, :] = jnp.zeros((LANE - rows, v32.shape[2]), F32)
         v32[z, :, 0:LANE] = jnp.zeros((LANE, LANE), F32)
@@ -139,41 +144,30 @@
             rc[it, k, ext:, :] = jnp.zeros((kext - ext, LANE), BF)
 
     up[...] = jnp.zeros_like(up)
+    ctf[...] = jnp.zeros_like(ctf)
     every = jnp.where(lax.rem(iota((WIN, LANE), 0), PITCH) == iota((WIN, LANE), 1), 1.0, 0.0)
     every = every.astype(BF)
-    y = s * rows + strip_row(iota((kext, LANE), 0))
-    inside = (y >= 0) & (y < rows * strips) & (iota((kext, LANE), 0) < ext)
-    inside = jnp.where(inside, 1.0, 0.0).astype(BF)
-    block = iota((16, WIN), 0)
-    xo = jnp.where(block < MOST, FIRST[0] + BW * block, FIRST[1] + BW * (block - MOST))
-    xo = xo + iota((16, WIN), 1)
-    xs = xo - RMAX
-    ones_win = jnp.where((xs >= 0) & (xs < cols), 1.0, 0.0).astype(BF)
-    col_ok = (xo < cols) & (iota((16, WIN), 1) < BW)
-    row_ok = iota((LANE, LANE), 0) < rows
     for copy in arg_in:
         copy.wait()
     for z in range(planes):
         reach = rad_ref[z]
-        ctf[...] = jnp.zeros_like(ctf)
         keep = jnp.abs(iota((PITCH, TAPS), 1) - RMAX) <= reach
-        ctf[0:PITCH, 0:TAPS] = jnp.where(keep, ct_ref[:, z, :], 0.0)
+        ctf[z, 0:PITCH, 0:TAPS] = jnp.where(keep, ct_ref[:, z, :], 0.0)
         keep1 = jnp.abs(iota((1, TAPS), 1) - RMAX) <= reach
-        ctf[16:17, 0:TAPS] = jnp.where(keep1, rt_ref[z : z + 1, :], 0.0)
+        ctf[z, 16:17, 0:TAPS] = jnp.where(keep1, rt_ref[z : z + 1, :], 0.0)
         family = jnp.full((16, LANE), -1, jnp.int32)
         for p in range(PITCH):
             family = jnp.where(iota((16, LANE), 0) == p, pm_ref[z, p], family)
         pick = jnp.where(family == iota((16, LANE), 1), 1.0, 0.0).astype(BF)
-        table = ctf[...].astype(BF)
-        up[0:16, :] = dot(pick, table)
-        taps = dot(every, up[...].astype(BF))
+        table = ctf[z].astype(BF)
+        up[z, 0:16, :] = dot(pick, table)
+        taps = dot(every, up[z].astype(BF))
+        tap_ref[z] = taps
         taps = jnp.concatenate([taps, jnp.zeros((WIN, WIN - LANE), F32)], axis=1)
         fwd = pltpu.roll(taps, 32 - 2 * RMAX, axis=1)
         fwd = pltpu.roll(fwd, WIN - 32, axis=1, stride=1, stride_axis=0)
         fm[z] = fwd.astype(BF)
-        back = pltpu.roll(taps, 0, axis=1, stride=1, stride_axis=0)
-        gm[z] = jnp.transpose(back).astype(BF)
-        rtap = jnp.concatenate([ctf[16:17, :], jnp.zeros((1, WIN - LANE), F32)], axis=1)
+        rtap = jnp.concatenate([ctf[z, 16:17, :], jnp.zeros((1, WIN - LANE), F32)], axis=1)
         rtap = jnp.broadcast_to(rtap, (LANE, WIN))
         band = pltpu.roll(rtap, 1, axis=1)
         band = pltpu.roll(band, 0, axis=1, stride=1, stride_axis=0)
@@ -183,14 +177,27 @@
         band = jnp.where(p < ext, band, 0.0)
         bt[z] = band[:, :kext].astype(BF)
         bfm[:, LANE * z : LANE * (z + 1)] = jnp.transpose(band)[:kext, :].astype(BF)
-        rn = dot(bt[z], inside)
-        rinv[z] = jnp.where(row_ok, 1.0 / rn, 0.0)
-        cn = dot(ones_win, gm[z])
-        cinv[z] = jnp.where(col_ok, 1.0 / cn, 0.0)
-
-    pl.semaphore_wait(barrier, 3 * chips)
-    for copy in mc_in:
-        copy.wait()
+
+    def back_operators():
+        y = s * rows + strip_row(iota((kext, LANE), 0))
+        inside = (y >= 0) & (y < rows * strips) & (iota((kext, LANE), 0) < ext)
+        inside = jnp.where(inside, 1.0, 0.0).astype(BF)
+        block = iota((16, WIN), 0)
+        xo = jnp.where(block < MOST, FIRST[0] + BW * block, FIRST[1] + BW * (block - MOST))
+        xo = xo + iota((16, WIN), 1)
+        xs = xo - RMAX
+        ones_win = jnp.where((xs >= 0) & (xs < cols), 1.0, 0.0).astype(BF)
+        col_ok = (xo < cols) & (iota((16, WIN), 1) < BW)
+        row_ok = iota((LANE, LANE), 0) < rows
+        for z in range(planes):
+            taps = jnp.concatenate([tap_ref[z], jnp.zeros((WIN, WIN - LANE), F32)], axis=1)
+            taps = pltpu.roll(taps, 0, axis=1, stride=1, stride_axis=0)
+            gm[z] = jnp.transpose(taps).astype(BF)
+            rn = dot(bt[z], inside)
+            rinv[z] = jnp.where(row_ok, 1.0 / rn, 0.0)
+            cn = dot(ones_win, gm[z])
+            cinv[z] = jnp.where(col_ok, 1.0 / cn, 0.0)
+
     def m_up(it):
         return pltpu.make_async_remote_copy(
             src_ref=mc.at[it, 3 * HALO : 4 * HALO, :], dst_ref=mc.at[it, HALO : 2 * HALO, :],
@@ -205,11 +212,13 @@
             device_id={"strip": below}, device_id_type=MESH,
         )
 
-    for it in range(ITERS):
-        m_up(it).start()
-        m_down(it).start()
-    for copy in vol_in:
-        copy.wait()
+    def meet():
+        pl.semaphore_wait(barrier, 3 * chips)
+        for copy in mc_in:
+            copy.wait()
+        for it in range(ITERS):
+            m_up(it).start()
+            m_down(it).start()
 
     def groups(count):
         return [(g, min(3, count - g)) for g in range(0, count, 3)]
@@ -226,6 +235,8 @@
         start = FIRST[q] + BW * first
 
         for z in range(planes):
+            if it == 0 and q == 0:
+                vol_in(z).wait()
             for g, n in groups(count):
                 lhs = jnp.concatenate([window(z, start + BW * (g + i)) for i in range(n)], axis=0)
                 res = dot(lhs, fm[z])
@@ -392,30 +403,31 @@
                     factor = jnp.where(x < hi, factor, 1.0)
                 v32[z, :, at] = v32[z, :, at] * factor
             if it == ITERS - 1 and q == 1:
-                pltpu.make_async_copy(
-                    v32.at[z, 0:rows, LANE : LANE + cols], out_hbm.at[z], sem_out.at[z]
-                ).start()
+                vol_out(z).start()
 
     def forward(it, q):
         spread(it, q)
         if it == 0 and q == 1:
             part_send(it, 0)
         sensor_part(it, q)
+        if it == 0 and q == 0:
+            meet()
         pair_send(it, q)
         if it > 0 or q == 1:
             part_send(it, q)
 
     forward(0, 0)
     forward(0, 1)
+    back_operators()
     for it in range(ITERS):
         ratio_send(it, 0)
         ratio_send(it, 1)
         ratio_forward(it, 0)
         ratio_arrived(it, 0)
         back(it, 0)
-        ratio_forward(it, 1)
         if it + 1 < ITERS:
             forward(it + 1, 0)
+        ratio_forward(it, 1)
         ratio_arrived(it, 1)
         back(it, 1)
         if it + 1 < ITERS:
@@ -439,9 +451,7 @@
                 for r in range(chips):
                     to_core(it, q, r).wait_send()
     for z in range(planes):
-        pltpu.make_async_copy(
-            v32.at[z, 0:rows, LANE : LANE + cols], out_hbm.at[z], sem_out.at[z]
-        ).wait()
+        vol_out(z).wait()
 
 
 def local(depths, strips, volume, measured, row_taps, col_taps, phase_map, radius):
@@ -475,8 +485,9 @@
             vmem((MOST * kext, WIN), BF),
             vmem((2, kext, MOST * WIN), BF),
             vmem((2, LANE, MOST * WIN), F32),
-            vmem((LANE, LANE), F32),
-            vmem((LANE, LANE), F32),
+            vmem((planes, LANE, LANE), F32),
+            vmem((planes, LANE, LANE), F32),
+            vmem((planes, WIN, LANE), F32),
             vmem((planes, WIN, WIN), BF),
             vmem((planes, WIN, WIN), BF),
             vmem((planes, LANE, kext), BF),

time: 52.7 us -> 52 us (0.987)
  Pallas kernels: 50.8 us -> 50.1 us
    pallas_call x1, Pallas kernels: 50.8 us -> 50.1 us  [local(): pl.pallas_call(functools.partial(kernel, depths, strips), out_shape=jax.S...]
where the time goes in v4:
time: 52 us; the launch traced here: 51.9 us
  Pallas kernels  50.1 us (96%)
  local copies, waits for them, and re-layouts  1.84 us (4%)
    pallas_call x1, Pallas kernels, local(): pl.pallas_call(functools.partial(kernel, depths, strips), out_shape=jax.S...  50.1 us
    unnamed x1, local copies, waits for them, and re-layouts  1.84 us

profile of v4, /device:TPU:1, one launch (start us, length us, event | category | flops | bytes accessed | tf_op | source)
XLA Modules:
  0.0 51.9 jit_solution(2397937390087864430)
XLA Ops:
  0.0 50.1 %shard_map.64 = f32[4,120,1920]{2,1,0:T(8,128)S(1)} custom-call(f32[4,120,1920]{2,1,0:T(8,128)} %vol_hbm.1, f32[120,1920]{1,0:T(8,128)} %meas_hbm.1, f32[4,31]{1,0:T(4,128)} %rt_hbm.1, f32[15,4,31]{2,1,0:T(4,128)} %bitcast.1, s32[4,15]{1,0:T(4,128)} %pm_hbm.1, s32[4]{0:T(128)} %rad_hbm.1), custom_call_target="tpu_custom_call" | custom-call | tf_op jit(solution)/shard_map/pallas_call | solution.py:465
  50.1 1.8 %copy.8 = f32[4,120,1920]{2,1,0:T(8,128)} copy(f32[4,120,1920]{2,1,0:T(8,128)S(1)} %shard_map.64) | data formatting | bytes 7372800

commit v5 on v4

--- a/solution.py
+++ b/solution.py
@@ -54,11 +54,11 @@
     return a
 
 
-def kernel(depths, strips, vol_hbm, meas_hbm, rt_hbm, ct_hbm, pm_hbm, rad_hbm, out_hbm,
+def kernel(depths, strips, vol_hbm, meas_hbm, rt_hbm, ct_hbm, pm_hbm, rad_hbm, out_ref,
            rt_ref, ct_ref, pm_ref, rad_ref,
            v32, spr, pw, pc, sb, qb, rb, ub, mc, rc, wr, ga, bpw,
            ctf, up, tap_ref, fm, gm, bt, bfm, cinv, rinv,
-           sem_vol, sem_out, sem_in, sem_ms, sem_mr, sem_ps, sem_pr, sem_rs, sem_rr,
+           sem_vol, sem_in, sem_ms, sem_mr, sem_ps, sem_pr, sem_rs, sem_rr,
            sem_hs, sem_hr, sem_as, sem_ar, sem_fs, sem_fr):
     planes, rows, cols = vol_hbm.shape
     ext = rows + 2 * HALO
@@ -106,11 +106,6 @@
     def vol_in(z):
         return pltpu.make_async_copy(
             vol_hbm.at[z], v32.at[z, 0:rows, LANE : LANE + cols], sem_vol.at[z]
-        )
-
-    def vol_out(z):
-        return pltpu.make_async_copy(
-            v32.at[z, 0:rows, LANE : LANE + cols], out_hbm.at[z], sem_out.at[z]
         )
 
     for z in range(planes):
@@ -401,9 +396,11 @@
                     factor = jnp.where(x >= lo, factor, 1.0)
                 if LANE * (k + 1) > hi:
                     factor = jnp.where(x < hi, factor, 1.0)
-                v32[z, :, at] = v32[z, :, at] * factor
-            if it == ITERS - 1 and q == 1:
-                vol_out(z).start()
+                new = v32[z, :, at] * factor
+                if it == ITERS - 1 and LANE * (k + 1) <= hi:
+                    out_ref[z, :, LANE * k : LANE * (k + 1)] = new[:rows]
+                else:
+                    v32[z, :, at] = new
 
     def forward(it, q):
         spread(it, q)
@@ -450,8 +447,6 @@
                     to_chip(it, q, r).wait_send()
                 for r in range(chips):
                     to_core(it, q, r).wait_send()
-    for z in range(planes):
-        vol_out(z).wait()
 
 
 def local(depths, strips, volume, measured, row_taps, col_taps, phase_map, radius):
@@ -466,7 +461,7 @@
         functools.partial(kernel, depths, strips),
         out_shape=jax.ShapeDtypeStruct(volume.shape, F32),
         in_specs=[pl.BlockSpec(memory_space=pltpu.HBM)] * 6,
-        out_specs=pl.BlockSpec(memory_space=pl.ANY),
+        out_specs=pl.BlockSpec(memory_space=pltpu.VMEM),
         scratch_shapes=[
             vmem(row_taps.shape, F32),
             vmem((PITCH, planes, TAPS), F32),
@@ -495,7 +490,6 @@
             vmem((planes, 16, WIN), F32),
             vmem((planes, LANE, LANE), F32),
             dma((planes,)),
-            dma((planes,)),
             dma((4 + 2 * ITERS,)),
             dma((ITERS, 2)),
             dma((ITERS, 2)),

time: 52 us -> 50.5 us (0.971)
  Pallas kernels: 50.1 us -> 48.5 us
    pallas_call x1, Pallas kernels: 50.1 us -> 48.5 us  [local(): pl.pallas_call(functools.partial(kernel, depths, strips), out_shape=jax.S...]
where the time goes in v5:
time: 50.5 us; the launch traced here: 50.4 us
  Pallas kernels  48.5 us (96%)
  local copies, waits for them, and re-layouts  1.84 us (4%)
    pallas_call x1, Pallas kernels, local(): pl.pallas_call(functools.partial(kernel, depths, strips), out_shape=jax.S...  48.5 us
    unnamed x1, local copies, waits for them, and re-layouts  1.84 us

profile of v5, /device:TPU:1, one launch (start us, length us, event | category | flops | bytes accessed | tf_op | source)
XLA Modules:
  0.0 50.4 jit_solution(8219070472254282320)
XLA Ops:
  0.0 48.5 %shard_map.64 = f32[4,120,1920]{2,1,0:T(8,128)S(1)} custom-call(f32[4,120,1920]{2,1,0:T(8,128)} %vol_hbm.1, f32[120,1920]{1,0:T(8,128)} %meas_hbm.1, f32[4,31]{1,0:T(4,128)} %rt_hbm.1, f32[15,4,31]{2,1,0:T(4,128)} %bitcast.1, s32[4,15]{1,0:T(4,128)} %pm_hbm.1, s32[4]{0:T(128)} %rad_hbm.1), custom_call_target="tpu_custom_call" | custom-call | tf_op jit(solution)/shard_map/pallas_call | solution.py:460
  48.5 1.8 %copy.8 = f32[4,120,1920]{2,1,0:T(8,128)} copy(f32[4,120,1920]{2,1,0:T(8,128)S(1)} %shard_map.64) | data formatting | bytes 7372800
